TPU v7x, 256 devices: a whole 4x4x8 slice. The times are simulated.
256 devices in a mesh: dp: 32 (over x, y, core), mp: 8 (over z).
Axes of the slice: x: 4, y: 4, z: 8, core: 2. Of those that a mesh axis runs over, the one named last changes fastest.
Arguments:
- features: bfloat16 [65536, 2, 512], P('dp'), may hold values from -27 to 27
- projection: bfloat16 [512, 256], replicated, may hold values from -1 to 1
- prototypes: float32 [3000, 256], P('mp'), may hold values from -7 to 7
Outputs:
- grad_prototypes: float32 [3000, 256], P('mp')
- grad_projection: float32 [512, 256], replicated
- loss: float32 [], replicated
All inputs are finite; a program needn't handle non-finite values.
Results may differ from a plain program's by a relative error of at most 0.0019.
The roundings to bfloat16 on the way count: a program that leaves them out, or rounds other values in their place, can miss the bound.
Values may be sent and summed in bfloat16 or wider, within the bound.
A program may use at most 128 MiB of HBM per device.

v0:
```python
import jax
import jax.numpy as jnp
from jax import lax
from jax.sharding import PartitionSpec as P

ITERS = 3
EPSILON_CODES = 0.05
SOFTMAX_TEMPER = 0.1
LOSS_FACTOR = 4096.0
TINY = 1e-06


def unit_rows(values):
    inverse = lax.rsqrt(jnp.sum(values * values, axis=-1, keepdims=True) + TINY)
    return (values * inverse, inverse)


def prototype_totals(values):
    return lax.psum(jnp.sum(values, axis=0), "dp")


def code_totals(values):
    return lax.psum(jnp.sum(values, axis=-1), "mp")


def loss_pieces(
    prototype_logits, softmax_exponent, softmax_denominator, assignments, gradient_factor
):
    swapped_targets = assignments[:, ::-1]
    grad_half = (
        (softmax_exponent / softmax_denominator[..., None] - swapped_targets) * gradient_factor
    ).astype(jnp.bfloat16)
    loss_portion = jnp.sum(
        swapped_targets
        * (prototype_logits * (1.0 / SOFTMAX_TEMPER) - jnp.log(softmax_denominator)[..., None])
    )
    return (grad_half, loss_portion)


def embed_backward(grad_unit, embed_unit, embed_inverse, own_feats):
    along_unit = jnp.sum(embed_unit * grad_unit, axis=-1, keepdims=True)
    grad_raw = ((grad_unit - embed_unit * along_unit) * embed_inverse).astype(jnp.bfloat16)
    return jnp.einsum("bve,bvp->ep", own_feats, grad_raw, preferred_element_type=jnp.float32)


def body(features, projection, prototypes):
    local_rows = features.shape[0]
    own_count = local_rows // lax.axis_size("mp")
    batch_row_count = local_rows * lax.axis_size("dp")
    gradient_factor = LOSS_FACTOR / (2.0 * batch_row_count * SOFTMAX_TEMPER)
    proto_unit, proto_inverse = unit_rows(prototypes)
    proto_half = proto_unit.astype(jnp.bfloat16)
    first_row = lax.axis_index("mp") * own_count
    own_feats = lax.dynamic_slice_in_dim(features, first_row, own_count, 0)
    raw_embed = jnp.einsum("bve,ep->bvp", own_feats, projection, preferred_element_type=jnp.float32)
    embed_unit, embed_inverse = unit_rows(raw_embed)
    embed_half = embed_unit.astype(jnp.bfloat16)
    all_embed = lax.all_gather(embed_half, "mp", axis=0, tiled=True)
    prototype_logits = jnp.einsum(
        "bvp,kp->bvk", all_embed, proto_half, preferred_element_type=jnp.float32
    )
    transport = jnp.exp(prototype_logits * (1.0 / EPSILON_CODES))
    softmax_exponent = jnp.exp(prototype_logits * (1.0 / SOFTMAX_TEMPER))
    soft_part = jnp.sum(softmax_exponent, axis=-1)
    for iteration in range(ITERS - 1):
        transport = transport / prototype_totals(transport)[None]
        transport = transport / code_totals(transport)[..., None]
    transport = transport / prototype_totals(transport)[None]
    softmax_denominator = lax.psum(soft_part, "mp")
    row_sums = code_totals(transport)
    assignments = transport / row_sums[..., None]
    grad_half, loss_portion = loss_pieces(
        prototype_logits, softmax_exponent, softmax_denominator, assignments, gradient_factor
    )
    proto_grad = jnp.einsum("bvk,bvp->kp", grad_half, all_embed, preferred_element_type=jnp.float32)
    proto_grad = lax.psum(proto_grad, "dp")
    grad_unit = lax.psum_scatter(
        jnp.einsum("bvk,kp->bvp", grad_half, proto_half, preferred_element_type=jnp.float32),
        "mp",
        scatter_dimension=0,
        tiled=True,
    )
    weight_part = embed_backward(grad_unit, embed_unit, embed_inverse, own_feats)
    weight_grad, loss_total = lax.psum((weight_part, loss_portion), ("dp", "mp"))
    along_proto = jnp.sum(proto_unit * proto_grad, axis=-1, keepdims=True)
    grad_protos = (proto_grad - proto_unit * along_proto) * proto_inverse
    loss_value = -loss_total / (2.0 * batch_row_count)
    return (grad_protos, weight_grad, loss_value)


def solution(mesh):
    return jax.shard_map(
        body,
        mesh=mesh,
        in_specs=(P("dp", None, None), P(), P("mp", None)),
        out_specs=(P("mp", None), P(), P()),
        check_vma=False,
    )
```

profile of v0, /device:TPU:2, one launch (start us, length us, event | category | flops | bytes accessed | tf_op | source)
XLA Modules:
  0.0 803.6 jit_solution(7048572155357733132)
XLA Ops:
  7.2 0.0 copy-start
  7.2 0.0 all-gather.2.cloned.1.call-start
  7.2 1.4 constant_dynamic-slice_fusion
  8.7 0.0 copy-start.3
  8.7 0.8 copy-done.3
  9.5 0.0 copy-done
  9.5 0.4 multiply_reduce_fusion.1
  9.9 0.7 multiply_convert_fusion.1
  10.6 0.0 all-gather.2.cloned.1.call-update
  10.6 0.0 reduce-scatter.2.cloned.1.call-start
  10.7 1.1 multiply_reduce_fusion.4
  11.8 49.1 %all-gather.2.cloned.1.call-done = bf16[2048,2,256]{0,2,1:T(8,128)(2,1)} async-done(((bf16[256,2,256]{0,2,1:T(8,128)(2,1)}), bf16[2048,2,256]{0,2,1:T(8,128)(2,1)}) %all-gather.2.cloned.1.call-update) | async-done | bytes 2097168 | tf_op jit(solution)/shard_map/all_gather | solution.py:58
  60.9 5.4 fusion.12
  66.3 53.0 %psum.71 = f32[2,375]{1,0:T(2,128)S(1)} all-reduce(f32[2,375]{1,0:T(2,128)S(1)} %get-tuple-element.11), channel_id=1, replica_groups=mesh['dp'=32,'mp'=8] {'dp'}, use_global_device_ids=true, to_apply=%region_5.0 | all-reduce | flops 750 | bytes 6000 | tf_op jit(solution)/shard_map/psum | solution.py:19
  119.3 3.8 exponential_reduce_fusion
  123.2 29.9 %psum.72 = f32[2048,2]{0,1:T(2,128)S(1)} all-reduce(f32[2048,2]{0,1:T(2,128)S(1)} %get-tuple-element.4), channel_id=1, replica_groups=mesh['dp'=32,'mp'=8] {'mp'}, use_global_device_ids=true, to_apply=%region_7.0 | all-reduce | flops 4096 | bytes 32768 | tf_op jit(solution)/shard_map/psum | solution.py:23
  153.0 4.4 fusion.8
  157.5 54.7 %psum.73 = f32[2,375]{1,0:T(2,128)S(1)} all-reduce(f32[2,375]{1,0:T(2,128)S(1)} %fusion.8), channel_id=1, replica_groups=mesh['dp'=32,'mp'=8] {'dp'}, use_global_device_ids=true, to_apply=%region_9.0 | all-reduce | flops 750 | bytes 6000 | tf_op jit(solution)/shard_map/psum | solution.py:19
  212.1 3.7 fusion.9
  215.9 27.0 %psum.74 = f32[2048,2]{0,1:T(2,128)S(1)} all-reduce(f32[2048,2]{0,1:T(2,128)S(1)} %fusion.9), channel_id=1, replica_groups=mesh['dp'=32,'mp'=8] {'mp'}, use_global_device_ids=true, to_apply=%region_11.0 | all-reduce | flops 4096 | bytes 32768 | tf_op jit(solution)/shard_map/psum | solution.py:23
  242.9 3.9 fusion.10
  246.8 62.7 %psum.75 = f32[2,375]{1,0:T(2,128)S(1)} all-reduce(f32[2,375]{1,0:T(2,128)S(1)} %fusion.10), channel_id=1, replica_groups=mesh['dp'=32,'mp'=8] {'dp'}, use_global_device_ids=true, to_apply=%region_13.0 | all-reduce | flops 750 | bytes 6000 | tf_op jit(solution)/shard_map/psum | solution.py:19
  309.5 0.0 slice-start
  309.5 4.3 fusion.11
  313.8 27.7 %all-reduce = (f32[2048,2]{0,1:T(2,128)S(1)}, f32[2048,2]{0,1:T(2,128)S(1)}) all-reduce(f32[2048,2]{0,1:T(2,128)S(1)} %fusion.11, f32[2048,2]{0,1:T(2,128)S(1)} %get-tuple-element.3), channel_id=1, replica_groups=mesh['dp'=32,'mp'=8] {'mp'}, use_global_device_ids=true, to_apply=%region_15.0 | all-reduce | flops 8192 | bytes 65536 | tf_op jit(solution)/shard_map/psum | solution.py:23
  341.5 0.0 slice-start.1
  341.5 5.1 fusion.7
  346.6 0.0 slice-done
  346.6 0.0 slice-done.1
  346.7 0.0 copy-start.2
  346.7 2.6 multiply_reduce_fusion
  349.2 0.0 copy-start.1
  349.2 1.6 copy-done.1
  350.9 0.0 copy-done.2
  350.9 3.3 fusion.28
  354.2 0.0 copy-start.4
  354.2 0.0 reduce-scatter.2.cloned.1.call-update
  354.2 0.0 all-reduce.4.cloned.1.call-start
  354.3 4.3 convolution_bitcast_fusion.1
  358.6 0.0 all-reduce.4.cloned.1.call-update
  358.7 0.0 all-reduce.6.cloned.1.call-start
  358.7 90.6 %psum.79 = f32[]{:T(128)} all-reduce(f32[]{:T(128)} %get-tuple-element.7), channel_id=1, replica_groups=mesh['dp'=32,'mp'=8] {'dp','mp'}, use_global_device_ids=true, to_apply=%region_22.0 | all-reduce | flops 1 | bytes 8 | tf_op jit(solution)/shard_map/psum | solution.py:84
  449.9 0.0 reduce-scatter.2.cloned.1.call-done
  450.0 0.0 copy-done.4
  450.0 2.5 convolution_bitcast_fusion
  452.5 0.0 all-reduce.6.cloned.1.call-update
  452.5 83.7 %all-reduce.4.cloned.1.call-done = f32[375,256]{1,0:T(8,128)} async-done(((f32[375,256]{1,0:T(8,128)}), f32[375,256]{1,0:T(8,128)}) %all-reduce.4.cloned.1.call-update) | async-done | bytes 384016 | tf_op jit(solution)/shard_map/psum | solution.py:76
  536.2 1.2 multiply_reduce_fusion.3
  537.4 1.9 subtract_multiply_fusion
  539.3 254.8 %all-reduce.6.cloned.1.call-done = f32[512,256]{1,0:T(8,128)} async-done(((f32[512,256]{1,0:T(8,128)}), f32[512,256]{1,0:T(8,128)}) %all-reduce.6.cloned.1.call-update) | async-done | bytes 524304 | tf_op jit(solution)/shard_map/psum | solution.py:84
  794.1 1.9 copy.29
  (4 shorter events, 0.0 us)
Async XLA Ops:
  7.2 2.3 copy-start
  7.2 53.7 %all-gather.2.cloned.1.call-start = ((), (), s32[]{:S(2)}) async-start(), calls=%async_computation.1 | async-start | bytes 2359296 | tf_op jit(solution)/shard_map/all_gather | solution.py:58
  8.7 0.8 copy-start.3
  10.6 439.3 %reduce-scatter.2.cloned.1.call-start = ((), (), s32[]{:S(2)}) async-start(), calls=%async_computation.3 | async-start | bytes 4718592 | tf_op jit(solution)/shard_map/reduce_scatter | solution.py:77
  309.5 37.1 %slice-start = ((s8[6160384]{0:T(1024)(128)(4,1)}), s8[1966080]{0:T(1024)(128)(4,1)S(1)}, s32[]{:S(2)}) async-start(s8[6160384]{0:T(1024)(128)(4,1)} %bitcast.19), calls=%async_computation.5 | async-start | bytes 3932160
  341.5 5.1 slice-start.1
  346.7 4.2 copy-start.2
  349.2 1.6 copy-start.1
  354.2 95.8 %copy-start.4 = (bf16[256,2,512]{2,1,0:T(2,128)(2,1)S(1)}, bf16[256,2,512]{2,1,0:T(2,128)(2,1)}, u32[]{:S(2)}) copy-start(bf16[256,2,512]{2,1,0:T(2,128)(2,1)} %copy-done.3) | copy-start | bytes 1572868
  354.2 181.9 %all-reduce.4.cloned.1.call-start = ((), (), s32[]{:S(2)}) async-start(), calls=%async_computation.2 | async-start | bytes 770048 | tf_op jit(solution)/shard_map/psum | solution.py:76
  358.7 435.4 %all-reduce.6.cloned.1.call-start = ((), (), s32[]{:S(2)}) async-start(), calls=%async_computation.4 | async-start | bytes 1048576 | tf_op jit(solution)/shard_map/psum | solution.py:84
Sparse Core Ops, SparseCore 0:
  10.7 50.1 all-gather.1
  354.4 66.9 reduce-scatter.1
  425.2 110.8 all-reduce.3
  542.1 251.9 all-reduce.5
where the time goes:
time: 804 us
  waiting for transfers between devices  388 us (48%)
  blocking collectives  345 us (43%)
  other arithmetic  32.9 us (4%)
  matrix products  16 us (2%)
  between operations  15.7 us (2%)
    psum x1, waiting for transfers between devices, body(): lax.psum((weight_part, loss_portion), ('dp', 'mp'))  255 us
    psum x3, blocking collectives, prototype_totals(): return lax.psum(jnp.sum(values, axis=0), 'dp')  170 us
    psum x1, blocking collectives, body(): lax.psum((weight_part, loss_portion), ('dp', 'mp'))  90.6 us
    psum x3, blocking collectives, code_totals(): return lax.psum(jnp.sum(values, axis=-1), 'mp')  84.6 us
    psum x1, waiting for transfers between devices, body(): proto_grad = lax.psum(proto_grad, 'dp')  83.7 us
    all_gather x1, waiting for transfers between devices, body(): all_embed = lax.all_gather(embed_half, 'mp', axis=0, tiled=True)  49.1 us
  transfers between devices with their start and end apart: 4, of which 3 were waited for; matrix products, arithmetic and copies ran while one was open for 1% of the time, Pallas kernels for 0%

commit v1 on v0

--- a/solution.py
+++ b/solution.py
@@ -73,7 +73,7 @@
         prototype_logits, softmax_exponent, softmax_denominator, assignments, gradient_factor
     )
     proto_grad = jnp.einsum("bvk,bvp->kp", grad_half, all_embed, preferred_element_type=jnp.float32)
-    proto_grad = lax.psum(proto_grad, "dp")
+    proto_grad = jnp.sum(lax.all_gather(proto_grad, "dp"), axis=0)
     grad_unit = lax.psum_scatter(
         jnp.einsum("bvk,kp->bvp", grad_half, proto_half, preferred_element_type=jnp.float32),
         "mp",

time: 804 us -> 758 us (0.943)
  waiting for transfers between devices: 388 us -> 338 us
    psum x1 -> x0, waiting for transfers between devices: 83.7 us -> none  [body(): proto_grad = lax.psum(proto_grad, 'dp')]
    all_gather x0 -> x1, waiting for transfers between devices: none -> 37.5 us  [body(): proto_grad = jnp.sum(lax.all_gather(proto_grad, 'dp'), axis=0)]
  transfers between devices with their start and end apart: 4 -> 4, of which waited for: 3 -> 3; matrix products, arithmetic and copies ran while one was open for 1% -> 2% of each run, Pallas kernels for 0% -> 0%
where the time goes in v1:
time: 758 us; the launch traced here: 757 us
  blocking collectives  346 us (46%)
  waiting for transfers between devices  338 us (45%)
  other arithmetic  36.3 us (5%)
  matrix products  16 us (2%)
  between operations  15.7 us (2%)
    psum x1, waiting for transfers between devices, body(): lax.psum((weight_part, loss_portion), ('dp', 'mp'))  251 us
    psum x3, blocking collectives, prototype_totals(): return lax.psum(jnp.sum(values, axis=0), 'dp')  170 us
    psum x1, blocking collectives, body(): lax.psum((weight_part, loss_portion), ('dp', 'mp'))  91 us
    psum x3, blocking collectives, code_totals(): return lax.psum(jnp.sum(values, axis=-1), 'mp')  84.6 us
    all_gather x1, waiting for transfers between devices, body(): all_embed = lax.all_gather(embed_half, 'mp', axis=0, tiled=True)  49.1 us
    all_gather x1, waiting for transfers between devices, body(): proto_grad = jnp.sum(lax.all_gather(proto_grad, 'dp'), axis=0)  37.5 us
  transfers between devices with their start and end apart: 4, of which 3 were waited for; matrix products, arithmetic and copies ran while one was open for 2% of the time, Pallas kernels for 0%

profile of v1, /device:TPU:2, one launch (start us, length us, event | category | flops | bytes accessed | tf_op | source)
XLA Modules:
  0.0 757.4 jit_solution(5588276538945294152)
XLA Ops:
  7.2 0.0 copy-start
  7.2 0.0 all-gather.5.cloned.1.call-start
  7.2 1.4 constant_dynamic-slice_fusion
  8.7 0.0 copy-start.3
  8.7 0.8 copy-done.3
  9.5 0.0 copy-done
  9.5 0.4 multiply_reduce_fusion.1
  9.9 0.7 multiply_convert_fusion.1
  10.6 0.0 all-gather.5.cloned.1.call-update
  10.6 0.0 reduce-scatter.2.cloned.1.call-start
  10.7 1.1 multiply_reduce_fusion.4
  11.8 49.1 %all-gather.5.cloned.1.call-done = bf16[2048,2,256]{0,2,1:T(8,128)(2,1)} async-done(((bf16[256,2,256]{0,2,1:T(8,128)(2,1)}), bf16[2048,2,256]{0,2,1:T(8,128)(2,1)}) %all-gather.5.cloned.1.call-update) | async-done | bytes 2097168 | tf_op jit(solution)/shard_map/all_gather | solution.py:58
  60.9 5.4 fusion.12
  66.3 53.0 %psum.64 = f32[2,375]{1,0:T(2,128)S(1)} all-reduce(f32[2,375]{1,0:T(2,128)S(1)} %get-tuple-element.11), channel_id=1, replica_groups=mesh['dp'=32,'mp'=8] {'dp'}, use_global_device_ids=true, to_apply=%region_5.0 | all-reduce | flops 750 | bytes 6000 | tf_op jit(solution)/shard_map/psum | solution.py:19
  119.3 3.8 exponential_reduce_fusion
  123.2 29.9 %psum.65 = f32[2048,2]{0,1:T(2,128)S(1)} all-reduce(f32[2048,2]{0,1:T(2,128)S(1)} %get-tuple-element.4), channel_id=1, replica_groups=mesh['dp'=32,'mp'=8] {'mp'}, use_global_device_ids=true, to_apply=%region_7.0 | all-reduce | flops 4096 | bytes 32768 | tf_op jit(solution)/shard_map/psum | solution.py:23
  153.0 4.4 fusion.8
  157.5 54.7 %psum.66 = f32[2,375]{1,0:T(2,128)S(1)} all-reduce(f32[2,375]{1,0:T(2,128)S(1)} %fusion.8), channel_id=1, replica_groups=mesh['dp'=32,'mp'=8] {'dp'}, use_global_device_ids=true, to_apply=%region_9.0 | all-reduce | flops 750 | bytes 6000 | tf_op jit(solution)/shard_map/psum | solution.py:19
  212.1 3.7 fusion.9
  215.9 27.0 %psum.67 = f32[2048,2]{0,1:T(2,128)S(1)} all-reduce(f32[2048,2]{0,1:T(2,128)S(1)} %fusion.9), channel_id=1, replica_groups=mesh['dp'=32,'mp'=8] {'mp'}, use_global_device_ids=true, to_apply=%region_11.0 | all-reduce | flops 4096 | bytes 32768 | tf_op jit(solution)/shard_map/psum | solution.py:23
  242.9 3.9 fusion.10
  246.8 62.7 %psum.68 = f32[2,375]{1,0:T(2,128)S(1)} all-reduce(f32[2,375]{1,0:T(2,128)S(1)} %fusion.10), channel_id=1, replica_groups=mesh['dp'=32,'mp'=8] {'dp'}, use_global_device_ids=true, to_apply=%region_13.0 | all-reduce | flops 750 | bytes 6000 | tf_op jit(solution)/shard_map/psum | solution.py:19
  309.5 0.0 slice-start
  309.5 4.3 fusion.11
  313.8 27.7 %all-reduce = (f32[2048,2]{0,1:T(2,128)S(1)}, f32[2048,2]{0,1:T(2,128)S(1)}) all-reduce(f32[2048,2]{0,1:T(2,128)S(1)} %fusion.11, f32[2048,2]{0,1:T(2,128)S(1)} %get-tuple-element.3), channel_id=1, replica_groups=mesh['dp'=32,'mp'=8] {'mp'}, use_global_device_ids=true, to_apply=%region_15.0 | all-reduce | flops 8192 | bytes 65536 | tf_op jit(solution)/shard_map/psum | solution.py:23
  341.5 0.0 slice-start.1
  341.5 5.1 fusion.7
  346.6 0.0 slice-done
  346.6 0.0 slice-done.1
  346.7 0.0 copy-start.2
  346.7 2.6 multiply_reduce_fusion
  349.2 0.0 copy-start.1
  349.2 1.6 copy-done.1
  350.9 0.0 copy-done.2
  350.9 3.4 fusion.28
  354.3 0.0 copy-start.4
  354.3 0.0 reduce-scatter.2.cloned.1.call-update
  354.3 0.0 all-gather.7.cloned.1.call-start
  354.3 4.3 convolution_bitcast_fusion.1
  358.7 0.0 all-gather.7.cloned.1.call-update
  358.7 0.0 all-reduce.3.cloned.1.call-start
  358.7 91.0 %psum.71 = f32[]{:T(128)} all-reduce(f32[]{:T(128)} %get-tuple-element.7), channel_id=1, replica_groups=mesh['dp'=32,'mp'=8] {'dp','mp'}, use_global_device_ids=true, to_apply=%region_22.0 | all-reduce | flops 1 | bytes 8 | tf_op jit(solution)/shard_map/psum | solution.py:84
  450.4 0.0 reduce-scatter.2.cloned.1.call-done
  450.4 0.0 copy-done.4
  450.4 2.5 convolution_bitcast_fusion
  452.9 0.0 all-reduce.3.cloned.1.call-update
  452.9 37.5 %all-gather.7.cloned.1.call-done = f32[32,375,256]{2,1,0:T(8,128)} async-done(((f32[1,375,256]{2,1,0:T(8,128)}), f32[32,375,256]{2,1,0:T(8,128)}) %all-gather.7.cloned.1.call-update) | async-done | bytes 12288016 | tf_op jit(solution)/shard_map/all_gather | solution.py:76
  490.4 5.3 reduce_sum.126
  495.8 0.2 multiply_reduce_fusion.3
  496.0 0.9 subtract_multiply_fusion
  496.9 251.0 %all-reduce.3.cloned.1.call-done = f32[512,256]{1,0:T(8,128)} async-done(((f32[512,256]{1,0:T(8,128)}), f32[512,256]{1,0:T(8,128)}) %all-reduce.3.cloned.1.call-update) | async-done | bytes 524304 | tf_op jit(solution)/shard_map/psum | solution.py:84
  747.9 1.9 copy.35
  (4 shorter events, 0.0 us)
Async XLA Ops:
  7.2 2.3 copy-start
  7.2 53.7 %all-gather.5.cloned.1.call-start = ((), (), s32[]{:S(2)}) async-start(), calls=%async_computation.1 | async-start | bytes 2359296 | tf_op jit(solution)/shard_map/all_gather | solution.py:58
  8.7 0.8 copy-start.3
  10.6 439.8 %reduce-scatter.2.cloned.1.call-start = ((), (), s32[]{:S(2)}) async-start(), calls=%async_computation.2 | async-start | bytes 4718592 | tf_op jit(solution)/shard_map/reduce_scatter | solution.py:77
  309.5 37.1 %slice-start = ((s8[6160384]{0:T(1024)(128)(4,1)}), s8[1966080]{0:T(1024)(128)(4,1)S(1)}, s32[]{:S(2)}) async-start(s8[6160384]{0:T(1024)(128)(4,1)} %bitcast.20), calls=%async_computation.5 | async-start | bytes 3932160
  341.5 5.1 slice-start.1
  346.7 4.2 copy-start.2
  349.2 1.6 copy-start.1
  354.3 96.1 %copy-start.4 = (bf16[256,2,512]{2,1,0:T(2,128)(2,1)S(1)}, bf16[256,2,512]{2,1,0:T(2,128)(2,1)}, u32[]{:S(2)}) copy-start(bf16[256,2,512]{2,1,0:T(2,128)(2,1)} %copy-done.3) | copy-start | bytes 1572868
  354.3 136.2 %all-gather.7.cloned.1.call-start = ((), (), s32[]{:S(2)}) async-start(), calls=%async_computation.4 | async-start | bytes 12705792 | tf_op jit(solution)/shard_map/all_gather | solution.py:76
  358.7 389.2 %all-reduce.3.cloned.1.call-start = ((), (), s32[]{:S(2)}) async-start(), calls=%async_computation.3 | async-start | bytes 1048576 | tf_op jit(solution)/shard_map/psum | solution.py:84
Sparse Core Ops, SparseCore 0:
  10.7 50.1 all-gather.4
  354.4 66.9 reduce-scatter.1
  424.6 65.8 all-gather.6
  496.3 251.5 all-reduce.2
